TPU v7x, 512 devices: a whole 4x4x16 slice. The times are simulated.
512 devices in a mesh: tile: 64 (over z, y_lo, core), inner: 8 (over x, y_hi).
Axes of the slice: x: 4, y: 4 (y_hi: 2, y_lo: 2; y = y_hi * 2 + y_lo), z: 16, core: 2. Of those that a mesh axis runs over, the one named last changes fastest.
Arguments:
- amplitudes: bfloat16 [512, 16384], P('tile', 'inner'), may hold values from -6 to 6
- left_factors: bfloat16 [1024, 16384], P('tile', 'inner'), may hold values from -0.1875 to 0.1875
- right_factors: bfloat16 [1024, 65536], P(None, 'tile'), may hold values from -0.1875 to 0.1875
- tile_pattern: int32 [32, 128], replicated, may hold values from 0 to 1, as said below
- occupied_shift: float32 [512], P('inner'), may hold values from 0.5 to 2
- virtual_shift: float32 [65536], P('tile'), may hold values from 0.5 to 5
Outputs:
- residual: float32 [512, 65536], P('inner', 'tile')
Inputs may be any that keep to these rules, and one draw needn't show every extreme that they name: `tile_pattern`: 1 where the tiles interact, 0 where their integrals are dropped.
All inputs are finite; a program needn't handle non-finite values.
Results may differ from a plain program's by a relative error of at most 0.0029.
Values may be sent and summed in bfloat16 or wider, within the bound.
A program may use at most 64 MiB of HBM per device.

v0:
```python
import jax
import jax.numpy as jnp
from jax import lax
from jax.sharding import Mesh
from jax.sharding import PartitionSpec as P

TILE = 512
TILE_AXES = ("tile_0", "tile_1", "tile_2")


def copy_for_each(shard, axis):
    peers = lax.axis_size(axis)
    return lax.all_to_all(
        jnp.broadcast_to(shard[None], (peers, *shard.shape)), axis, 0, 0, tiled=True
    )


def laid_out(pieces, dim):
    dims = list(pieces.shape[1:])
    dims[dim] *= pieces.shape[0]
    return jnp.moveaxis(pieces, 0, dim).reshape(dims)


def gather_axes(shard, axes, dim):
    far, near = axes
    leading = copy_for_each(shard, far)
    pieces = jnp.swapaxes(copy_for_each(leading, near), 0, 1)
    return laid_out(pieces.reshape(-1, *shard.shape), dim)


def split_up(shard, dim, peers):
    dims = shard.shape
    pieces = shard.reshape(*dims[:dim], peers, dims[dim] // peers, *dims[dim + 1 :])
    return jnp.moveaxis(pieces, dim, 0)


def sum_at_owner(shard, axis, dim):
    pieces = split_up(shard, dim, lax.axis_size(axis))
    arrived = lax.all_to_all(pieces, axis, split_axis=0, concat_axis=0, tiled=True)
    return arrived.sum(axis=0)


def on_device(amplitudes, left_factors, right_factors, tile_pattern, occupied_shift, virtual_shift):
    inner_place = lax.axis_index("inner")
    tile_place = lax.axis_index(TILE_AXES)
    block_width = amplitudes.shape[1]
    out_width = right_factors.shape[1]
    left_tiles = block_width // TILE
    right_tiles = out_width // TILE
    gathered_rows = gather_axes(amplitudes, (("tile_0", "tile_1"), "tile_2"), 0)
    local_mask = lax.dynamic_slice(
        tile_pattern,
        (inner_place * left_tiles, tile_place * right_tiles),
        (left_tiles, right_tiles),
    )
    factor_block = lax.all_gather(left_factors, TILE_AXES, axis=0, tiled=True)

    def integral_tile(left_slot, right_slot):
        left_cols = lax.dynamic_slice_in_dim(factor_block, left_slot * TILE, TILE, 1)
        right_cols = lax.dynamic_slice_in_dim(right_factors, right_slot * TILE, TILE, 1)
        return lax.dot_general(
            left_cols, right_cols, (((0,), (0,)), ((), ())), preferred_element_type=jnp.float32
        ).astype(jnp.bfloat16)

    def visit_tile(position, totals):
        left_slot = position // right_tiles
        right_slot = position % right_tiles

        def include(current):
            integral = integral_tile(left_slot, right_slot)
            amplitude_tile = lax.dynamic_slice_in_dim(gathered_rows, left_slot * TILE, TILE, 1)
            update = jnp.dot(amplitude_tile, integral, preferred_element_type=jnp.float32)
            column = lax.dynamic_slice_in_dim(current, right_slot * TILE, TILE, 1)
            return lax.dynamic_update_slice_in_dim(current, column + update, right_slot * TILE, 1)

        return lax.cond(
            local_mask[left_slot, right_slot] != 0, include, lambda current: current, totals
        )

    partial_sum = lax.fori_loop(
        0,
        left_tiles * right_tiles,
        visit_tile,
        jnp.zeros((gathered_rows.shape[0], out_width), jnp.float32),
    )
    summed = sum_at_owner(partial_sum, "inner", 0)
    return summed / (occupied_shift[:, None] + virtual_shift[None, :])


def solution(mesh):
    torus = Mesh(
        mesh.devices.reshape(16, 2, 2, mesh.shape["inner"]), ("tile_0", "tile_1", "tile_2", "inner")
    )
    placed = (
        P(TILE_AXES, "inner"),
        P(TILE_AXES, "inner"),
        P(None, TILE_AXES),
        P(),
        P("inner"),
        P(TILE_AXES),
    )
    return jax.shard_map(
        on_device, mesh=torus, in_specs=placed, out_specs=P("inner", TILE_AXES), check_vma=False
    )
```

profile of v0, /device:TPU:1, one launch (start us, length us, event | category | flops | bytes accessed | tf_op | source)
XLA Modules:
  0.0 223.0 jit_solution(12092331549922296120)
XLA Ops:
  7.3 1.8 broadcast_in_dim.7
  9.1 17.0 %all-to-all-start = ((bf16[32,8,2048]{2,1,0:T(8,128)(2,1)}), bf16[32,8,2048]{2,1,0:T(8,128)(2,1)S(1)}, u32[]{:S(2)}, u32[]{:S(2)}) async-start(bf16[32,8,2048]{2,1,0:T(8,128)(2,1)} %broadcast_in_dim.7), calls=%async_computation | async-start | bytes 2097152 | tf_op jit(solution)/shard_map/all_to_all | solution.py:13
  26.9 59.0 %all-to-all-done = bf16[32,8,2048]{2,1,0:T(8,128)(2,1)S(1)} async-done(((bf16[32,8,2048]{2,1,0:T(8,128)(2,1)}), bf16[32,8,2048]{2,1,0:T(8,128)(2,1)S(1)}, u32[]{:S(2)}, u32[]{:S(2)}) %all-to-all-start) | async-done | bytes 1048608 | tf_op jit(solution)/shard_map/all_to_all | solution.py:13
  86.1 8.8 %all_to_all.15 = bf16[2,32,8,2048]{3,2,1,0:T(8,128)(2,1)S(1)} all-to-all(bf16[2,32,8,2048]{3,2,1,0:T(8,128)(2,1)S(1)} %broadcast_in_dim.8), channel_id=1, replica_groups=mesh['tile_0'=16,'tile_1'=2,'tile_2'=2,'inner'=8] {'tile_2'}, dimensions={0} | all-to-all | bytes 4194304 | tf_op jit(solution)/shard_map/all_to_all | solution.py:13
  94.9 1.5 copy.10
  96.4 59.0 %all-gather.2.cloned.1.call-done = bf16[1024,2048]{1,0:T(8,128)(2,1)} async-done(((bf16[16,2048]{1,0:T(8,128)(2,1)}), bf16[1024,2048]{1,0:T(8,128)(2,1)}) %all-gather.2.cloned.1.call-update) | async-done | bytes 4194320 | tf_op jit(solution)/shard_map/all_gather | solution.py:56
  155.7 30.2 %while.18 = (s32[]{:T(128)}, f32[512,1024]{1,0:T(8,128)S(1)}, s32[4,2]{1,0:T(4,128)S(1)}, bf16[512,2048]{1,0:T(8,128)(2,1)}, bf16[1024,2048]{1,0:T(8,128)(2,1)},...) while((s32[]{:T(128)}, f32[512,1024]{1,0:T(8,128)S(1)}, ...), condition=%wide.region_3.4_spmd, body=%wide.region_0.3_spmd.sunk | while | flops 805830656 | bytes 4721122 | solution.py:80
  156.9 2.9 %conditional.2 = (f32[512,1024]{1,0:T(8,128)S(1)}) conditional(s32[]{:T(128)} %bitcast.9, f32[512,1024]{1,0:T(8,128)S(1)} %get-tuple-element.254, (s32[]{:T(128)}, f32[512,1024]{1,0:T(8,128)S(1)}, s32[]{:T(128)}, bf16[512,2048]{1,0:T(8,128)(2,1)}, bf16[1024,2048]{1,0:T(8,128)(2,1)}, /*index=5*/bf16[1024,1024]{1,0:T(8,128)(2,1)}) %tuple.50), branch_computations={%region_1.1_spmd, %region_2.2_spmd} | conditional | flops 805830656 | bytes 4720740 | solution.py:76
  156.9 2.8 %fusion = f32[512,1024]{1,0:T(8,128)S(1)} fusion(f32[512,1024]{1,0:T(8,128)S(1)} %get-tuple-element.177, s32[]{:T(128)S(6)} %select_n.59, bf16[1024,1024]{1,0:T(8,128)(2,1)} %get-tuple-element.182, bf16[1024,2048]{1,0:T(8,128)(2,1)} %get-tuple-element.181, s32[]{:T(128)S(6)} %select_n.60, bf16[512,2048]{1,0:T(8,128)(2,1)} %get-tuple-element.179), kind=kOutput, calls=%fused_computation.1 | convolution fusion | flops 805830656 | bytes 4720640 | tf_op jit(solution)/shard_map/while/body/eval_jaxpr/cond/branch_1_fun/dot_general | solution.py:72
  161.0 2.9 %conditional.2 = (f32[512,1024]{1,0:T(8,128)S(1)}) conditional(s32[]{:T(128)} %bitcast.9, f32[512,1024]{1,0:T(8,128)S(1)} %get-tuple-element.254, (s32[]{:T(128)}, f32[512,1024]{1,0:T(8,128)S(1)}, s32[]{:T(128)}, bf16[512,2048]{1,0:T(8,128)(2,1)}, bf16[1024,2048]{1,0:T(8,128)(2,1)}, /*index=5*/bf16[1024,1024]{1,0:T(8,128)(2,1)}) %tuple.50), branch_computations={%region_1.1_spmd, %region_2.2_spmd} | conditional | flops 805830656 | bytes 4720740 | solution.py:76
  161.1 2.8 %fusion = f32[512,1024]{1,0:T(8,128)S(1)} fusion(f32[512,1024]{1,0:T(8,128)S(1)} %get-tuple-element.177, s32[]{:T(128)S(6)} %select_n.59, bf16[1024,1024]{1,0:T(8,128)(2,1)} %get-tuple-element.182, bf16[1024,2048]{1,0:T(8,128)(2,1)} %get-tuple-element.181, s32[]{:T(128)S(6)} %select_n.60, bf16[512,2048]{1,0:T(8,128)(2,1)} %get-tuple-element.179), kind=kOutput, calls=%fused_computation.1 | convolution fusion | flops 805830656 | bytes 4720640 | tf_op jit(solution)/shard_map/while/body/eval_jaxpr/cond/branch_1_fun/dot_general | solution.py:72
  165.2 2.9 %conditional.2 = (f32[512,1024]{1,0:T(8,128)S(1)}) conditional(s32[]{:T(128)} %bitcast.9, f32[512,1024]{1,0:T(8,128)S(1)} %get-tuple-element.254, (s32[]{:T(128)}, f32[512,1024]{1,0:T(8,128)S(1)}, s32[]{:T(128)}, bf16[512,2048]{1,0:T(8,128)(2,1)}, bf16[1024,2048]{1,0:T(8,128)(2,1)}, /*index=5*/bf16[1024,1024]{1,0:T(8,128)(2,1)}) %tuple.50), branch_computations={%region_1.1_spmd, %region_2.2_spmd} | conditional | flops 805830656 | bytes 4720740 | solution.py:76
  165.2 2.8 %fusion = f32[512,1024]{1,0:T(8,128)S(1)} fusion(f32[512,1024]{1,0:T(8,128)S(1)} %get-tuple-element.177, s32[]{:T(128)S(6)} %select_n.59, bf16[1024,1024]{1,0:T(8,128)(2,1)} %get-tuple-element.182, bf16[1024,2048]{1,0:T(8,128)(2,1)} %get-tuple-element.181, s32[]{:T(128)S(6)} %select_n.60, bf16[512,2048]{1,0:T(8,128)(2,1)} %get-tuple-element.179), kind=kOutput, calls=%fused_computation.1 | convolution fusion | flops 805830656 | bytes 4720640 | tf_op jit(solution)/shard_map/while/body/eval_jaxpr/cond/branch_1_fun/dot_general | solution.py:72
  170.6 2.9 %conditional.2 = (f32[512,1024]{1,0:T(8,128)S(1)}) conditional(s32[]{:T(128)} %bitcast.9, f32[512,1024]{1,0:T(8,128)S(1)} %get-tuple-element.254, (s32[]{:T(128)}, f32[512,1024]{1,0:T(8,128)S(1)}, s32[]{:T(128)}, bf16[512,2048]{1,0:T(8,128)(2,1)}, bf16[1024,2048]{1,0:T(8,128)(2,1)}, /*index=5*/bf16[1024,1024]{1,0:T(8,128)(2,1)}) %tuple.50), branch_computations={%region_1.1_spmd, %region_2.2_spmd} | conditional | flops 805830656 | bytes 4720740 | solution.py:76
  170.6 2.8 %fusion = f32[512,1024]{1,0:T(8,128)S(1)} fusion(f32[512,1024]{1,0:T(8,128)S(1)} %get-tuple-element.177, s32[]{:T(128)S(6)} %select_n.59, bf16[1024,1024]{1,0:T(8,128)(2,1)} %get-tuple-element.182, bf16[1024,2048]{1,0:T(8,128)(2,1)} %get-tuple-element.181, s32[]{:T(128)S(6)} %select_n.60, bf16[512,2048]{1,0:T(8,128)(2,1)} %get-tuple-element.179), kind=kOutput, calls=%fused_computation.1 | convolution fusion | flops 805830656 | bytes 4720640 | tf_op jit(solution)/shard_map/while/body/eval_jaxpr/cond/branch_1_fun/dot_general | solution.py:72
  174.7 2.9 %conditional.2 = (f32[512,1024]{1,0:T(8,128)S(1)}) conditional(s32[]{:T(128)} %bitcast.9, f32[512,1024]{1,0:T(8,128)S(1)} %get-tuple-element.254, (s32[]{:T(128)}, f32[512,1024]{1,0:T(8,128)S(1)}, s32[]{:T(128)}, bf16[512,2048]{1,0:T(8,128)(2,1)}, bf16[1024,2048]{1,0:T(8,128)(2,1)}, /*index=5*/bf16[1024,1024]{1,0:T(8,128)(2,1)}) %tuple.50), branch_computations={%region_1.1_spmd, %region_2.2_spmd} | conditional | flops 805830656 | bytes 4720740 | solution.py:76
  174.8 2.8 %fusion = f32[512,1024]{1,0:T(8,128)S(1)} fusion(f32[512,1024]{1,0:T(8,128)S(1)} %get-tuple-element.177, s32[]{:T(128)S(6)} %select_n.59, bf16[1024,1024]{1,0:T(8,128)(2,1)} %get-tuple-element.182, bf16[1024,2048]{1,0:T(8,128)(2,1)} %get-tuple-element.181, s32[]{:T(128)S(6)} %select_n.60, bf16[512,2048]{1,0:T(8,128)(2,1)} %get-tuple-element.179), kind=kOutput, calls=%fused_computation.1 | convolution fusion | flops 805830656 | bytes 4720640 | tf_op jit(solution)/shard_map/while/body/eval_jaxpr/cond/branch_1_fun/dot_general | solution.py:72
  178.9 2.9 %conditional.2 = (f32[512,1024]{1,0:T(8,128)S(1)}) conditional(s32[]{:T(128)} %bitcast.9, f32[512,1024]{1,0:T(8,128)S(1)} %get-tuple-element.254, (s32[]{:T(128)}, f32[512,1024]{1,0:T(8,128)S(1)}, s32[]{:T(128)}, bf16[512,2048]{1,0:T(8,128)(2,1)}, bf16[1024,2048]{1,0:T(8,128)(2,1)}, /*index=5*/bf16[1024,1024]{1,0:T(8,128)(2,1)}) %tuple.50), branch_computations={%region_1.1_spmd, %region_2.2_spmd} | conditional | flops 805830656 | bytes 4720740 | solution.py:76
  178.9 2.8 %fusion = f32[512,1024]{1,0:T(8,128)S(1)} fusion(f32[512,1024]{1,0:T(8,128)S(1)} %get-tuple-element.177, s32[]{:T(128)S(6)} %select_n.59, bf16[1024,1024]{1,0:T(8,128)(2,1)} %get-tuple-element.182, bf16[1024,2048]{1,0:T(8,128)(2,1)} %get-tuple-element.181, s32[]{:T(128)S(6)} %select_n.60, bf16[512,2048]{1,0:T(8,128)(2,1)} %get-tuple-element.179), kind=kOutput, calls=%fused_computation.1 | convolution fusion | flops 805830656 | bytes 4720640 | tf_op jit(solution)/shard_map/while/body/eval_jaxpr/cond/branch_1_fun/dot_general | solution.py:72
  183.0 2.9 %conditional.2 = (f32[512,1024]{1,0:T(8,128)S(1)}) conditional(s32[]{:T(128)} %bitcast.9, f32[512,1024]{1,0:T(8,128)S(1)} %get-tuple-element.254, (s32[]{:T(128)}, f32[512,1024]{1,0:T(8,128)S(1)}, s32[]{:T(128)}, bf16[512,2048]{1,0:T(8,128)(2,1)}, bf16[1024,2048]{1,0:T(8,128)(2,1)}, /*index=5*/bf16[1024,1024]{1,0:T(8,128)(2,1)}) %tuple.50), branch_computations={%region_1.1_spmd, %region_2.2_spmd} | conditional | flops 805830656 | bytes 4720740 | solution.py:76
  183.0 2.8 %fusion = f32[512,1024]{1,0:T(8,128)S(1)} fusion(f32[512,1024]{1,0:T(8,128)S(1)} %get-tuple-element.177, s32[]{:T(128)S(6)} %select_n.59, bf16[1024,1024]{1,0:T(8,128)(2,1)} %get-tuple-element.182, bf16[1024,2048]{1,0:T(8,128)(2,1)} %get-tuple-element.181, s32[]{:T(128)S(6)} %select_n.60, bf16[512,2048]{1,0:T(8,128)(2,1)} %get-tuple-element.179), kind=kOutput, calls=%fused_computation.1 | convolution fusion | flops 805830656 | bytes 4720640 | tf_op jit(solution)/shard_map/while/body/eval_jaxpr/cond/branch_1_fun/dot_general | solution.py:72
  185.9 1.3 copy-done
  187.2 27.4 %all_to_all.16 = f32[8,64,1024]{2,1,0:T(8,128)S(1)} all-to-all(f32[8,64,1024]{2,1,0:T(8,128)} %bitcast.10), channel_id=1, replica_groups=mesh['tile_0'=16,'tile_1'=2,'tile_2'=2,'inner'=8] {'inner'}, dimensions={0} | all-to-all | bytes 4194304 | tf_op jit(solution)/shard_map/all_to_all | solution.py:39
  215.3 0.8 add_divide_fusion
  (20 shorter events, 7.5 us)
Async XLA Ops:
  6.5 148.9 %all-gather.2.cloned.1.call-start = ((), (), s32[]{:S(2)}) async-start(), calls=%async_computation.3 | async-start | bytes 4259840 | tf_op jit(solution)/shard_map/all_gather | solution.py:56
  9.1 76.8 %all-to-all-start = ((bf16[32,8,2048]{2,1,0:T(8,128)(2,1)}), bf16[32,8,2048]{2,1,0:T(8,128)(2,1)S(1)}, u32[]{:S(2)}, u32[]{:S(2)}) async-start(bf16[32,8,2048]{2,1,0:T(8,128)(2,1)} %broadcast_in_dim.7), calls=%async_computation | async-start | bytes 2097152 | tf_op jit(solution)/shard_map/all_to_all | solution.py:13
  185.9 1.3 copy-start
  214.6 0.7 copy-start.1
  214.6 0.7 copy-start.2
Sparse Core Ops, SparseCore 0:
  9.5 145.8 all-gather.1
where the time goes:
time: 223 us
  waiting for transfers between devices  119 us (53%)
  blocking collectives  36.2 us (16%)
  matrix products  19.9 us (9%)
  starting transfers between devices  17 us (8%)
  between operations  13.5 us (6%)
  local copies, waits for them, and re-layouts  11.2 us (5%)
  loops' own time  5.51 us (2%)
    all_gather x1, waiting for transfers between devices, on_device(): factor_block = lax.all_gather(left_factors, TILE_AXES, axis=0, tiled=True)  59 us
    all_to_all x1, waiting for transfers between devices, copy_for_each(): lax.all_to_all(jnp.broadcast_to(shard[None], (peers, *shard.shape)), axis...  59 us
    all_to_all x1, blocking collectives, sum_at_owner(): lax.all_to_all(pieces, axis, split_axis=0, concat_axis=0, tiled=True)  27.4 us
    dot_general x7, matrix products, include(): jnp.dot(amplitude_tile, integral, preferred_element_type=jnp.float32)  19.9 us
    all_to_all x1, starting transfers between devices, copy_for_each(): lax.all_to_all(jnp.broadcast_to(shard[None], (peers, *shard.shape)), axis...  17 us
    all_to_all x1, blocking collectives, copy_for_each(): lax.all_to_all(jnp.broadcast_to(shard[None], (peers, *shard.shape)), axis...  8.81 us
    another operation x1, loops' own time, on_device(): lax.fori_loop(0, left_tiles * right_tiles, visit_tile, jnp.zeros((gathere...  5.32 us
    dynamic_slice x8, local copies, waits for them, and re-layouts, visit_tile(): local_mask[left_slot, right_slot] != 0  4.8 us
  transfers between devices with their start and end apart: 2, of which 2 were waited for; matrix products, arithmetic and copies ran while one was open for 2% of the time, Pallas kernels for 0%

commit v1 on v0

v1 whole, which is shorter than its diff:
```python
import functools

import jax
import jax.numpy as jnp
from jax import lax
from jax.experimental import pallas as pl
from jax.experimental.pallas import tpu as pltpu
from jax.sharding import Mesh
from jax.sharding import PartitionSpec as P

TILE = 512
TILE_AXES = ("z", "y", "core")
MESH_ID = pl.DeviceIdType.MESH
PLANES = 16
INNER = 8
QUADS = 4
HALVES = 2
LEFT = 4
RIGHT = 128
ROWS = 8
DEPTH = 64
LANES = 128
GROUP = PLANES * QUADS


def kernel(
    a_ref, l_ref, r_ref, pattern_ref, out_ref,
    a_all, l_all, r_all, kron, m_out, m_in, s_out, s_in,
    ring_send, ring_recv, near_send, near_recv, m_send, m_recv, s_send, s_recv, own_sem,
):
    z = lax.axis_index("z")
    y = lax.axis_index("y")
    core = lax.axis_index("core")
    inner = lax.axis_index("inner")
    quad = y * 2 + core
    place = z * QUADS + quad
    pair = (z // 2) * 2
    parity = z % 2

    def tile_device(spot):
        return dict(z=spot // QUADS, y=(spot // 2) % 2, core=spot % 2, inner=inner)

    def mix_device(spot):
        return dict(z=pair + spot % 2, y=y, core=core, inner=spot // 2)

    mix_place = inner * 2 + parity
    barrier = pltpu.get_barrier_semaphore()

    @pl.loop(1, GROUP)
    def _(step):
        pl.semaphore_signal(
            barrier, 1, device_id=tile_device((place + step) % GROUP), device_id_type=MESH_ID
        )

    @pl.loop(0, INNER)
    def _(other):
        @pl.when(other != inner)
        def _():
            for side in range(2):
                pl.semaphore_signal(
                    barrier, 1, device_id=mix_device(other * 2 + side), device_id_type=MESH_ID
                )

    own_a = pltpu.make_async_copy(a_ref, a_all.at[z], own_sem.at[0])
    own_l = pltpu.make_async_copy(l_ref, l_all.at[quad], own_sem.at[1])
    own_r = pltpu.make_async_copy(r_ref, r_all, own_sem.at[2])
    own_a.start()
    own_l.start()
    own_r.start()
    pl.semaphore_wait(barrier, GROUP - 1 + 2 * (INNER - 1))

    span = a_ref.shape[1] // HALVES

    def hop(way, step, half):
        toward = 1 if way == 0 else PLANES - 1
        back = PLANES - step if way == 0 else step
        origin = (z + back) % PLANES
        columns = pl.ds(half * span, span)
        src = a_ref.at[:, columns] if step == 0 else a_all.at[origin, :, columns]
        return pltpu.make_async_remote_copy(
            src_ref=src,
            dst_ref=a_all.at[origin, :, columns],
            send_sem=ring_send.at[way, step, half],
            recv_sem=ring_recv.at[way, step, half],
            device_id=dict(z=(z + toward) % PLANES, y=y, core=core, inner=inner),
            device_id_type=MESH_ID,
        )

    def hops(step):
        if step < PLANES // 2 - 1:
            return [hop(way, step, half) for half in range(HALVES) for way in range(2)]
        return [hop(half, step, half) for half in range(HALVES)]

    ring = [hops(step) for step in range(PLANES // 2)]
    for copy in ring[0]:
        copy.start()

    def near_copy(step):
        other = (quad + step) % QUADS
        return pltpu.make_async_remote_copy(
            src_ref=l_ref,
            dst_ref=l_all.at[quad],
            send_sem=near_send.at[step - 1],
            recv_sem=near_recv.at[step - 1],
            device_id=dict(z=z, y=other // 2, core=other % 2, inner=inner),
            device_id_type=MESH_ID,
        )

    near = [near_copy(step) for step in range(1, QUADS)]
    for copy in near:
        copy.start()

    mask = jnp.where(pattern_ref[...] != 0, 1.0, 0.0).astype(jnp.bfloat16)
    spread = jnp.where(
        lax.broadcasted_iota(jnp.int32, (32, 256), 0)
        == lax.broadcasted_iota(jnp.int32, (32, 256), 1) >> 3,
        1.0,
        0.0,
    ).astype(jnp.bfloat16)
    spread = lax.dot_general(
        mask, spread, (((0,), (0,)), ((), ())), preferred_element_type=jnp.float32
    ).astype(jnp.bfloat16)
    same = jnp.where(
        (lax.broadcasted_iota(jnp.int32, (LANES, 256), 0) & 7)
        == (lax.broadcasted_iota(jnp.int32, (LANES, 256), 1) & 7),
        1.0,
        0.0,
    )
    lifted = lax.broadcasted_iota(jnp.int32, (LANES, RIGHT), 1) - (
        lax.broadcasted_iota(jnp.int32, (LANES, RIGHT), 0) >> 3
    )

    @pl.loop(0, RIGHT // 16)
    def _(block):
        lift = jnp.where(lifted == block * 16, 1.0, 0.0).astype(jnp.bfloat16)
        rows = jnp.dot(lift, spread, preferred_element_type=jnp.float32)
        kron[pl.ds(pl.multiple_of(block * LANES, LANES), LANES), :] = (rows * same).astype(
            jnp.bfloat16
        )

    for step in range(PLANES // 2 - 1):
        for now, later in zip(ring[step], ring[step + 1] if step < PLANES // 2 - 2 else [None] * 4):
            now.wait_recv()
            if later is not None:
                later.start()
        if step == PLANES // 2 - 2:
            for later in ring[step + 1]:
                later.start()
    for copy in ring[-1]:
        copy.wait_recv()
    own_a.wait()
    own_l.wait()
    for copy in near:
        copy.wait_recv()

    left_side = lax.broadcasted_iota(jnp.int32, (PLANES * ROWS, LANES), 1) < DEPTH
    for couple in range(LEFT // 2):
        wide = []
        for left in (couple * 2, couple * 2 + 1):
            columns = pl.ds(left * TILE, TILE)
            factors = l_all[:, :, columns].reshape(DEPTH, TILE)
            wide.append(
                lax.dot_general(
                    a_all[:, :, columns].reshape(PLANES * ROWS, TILE),
                    jnp.concatenate([factors, factors], axis=0),
                    (((1,), (1,)), ((), ())),
                    preferred_element_type=jnp.float32,
                )
            )
        m_out[:, couple] = jnp.where(left_side, *wide).reshape(PLANES, ROWS, LANES)

    def mix_copy(spot):
        return pltpu.make_async_remote_copy(
            src_ref=m_out.at[spot],
            dst_ref=m_in.at[mix_place],
            send_sem=m_send.at[spot],
            recv_sem=m_recv.at[mix_place],
            device_id=mix_device(spot),
            device_id_type=MESH_ID,
        )

    @pl.loop(1, 2 * INNER)
    def _(step):
        mix_copy((mix_place + step) % (2 * INNER)).start()

    m_in[mix_place] = m_out[mix_place]

    def mix_arrival(spot):
        return pltpu.make_async_remote_copy(
            src_ref=m_out.at[spot],
            dst_ref=m_in.at[spot],
            send_sem=m_send.at[spot],
            recv_sem=m_recv.at[spot],
            device_id=mix_device(spot),
            device_id_type=MESH_ID,
        )

    @pl.loop(1, 2 * INNER)
    def _(step):
        mix_arrival((mix_place + 2 * INNER - step) % (2 * INNER)).wait_recv()

    tall = m_in[...].reshape(INNER, 2, LEFT // 2, ROWS, LANES)
    even = tall[:, 0].reshape(INNER * LEFT // 2 * ROWS, LANES)
    odd = tall[:, 1].reshape(INNER * LEFT // 2 * ROWS, LANES)
    first = jnp.where(left_side, even, pltpu.roll(odd, DEPTH, 1))
    second = jnp.where(left_side, pltpu.roll(even, DEPTH, 1), odd)
    stacked = jnp.concatenate(
        [
            first.reshape(INNER * LEFT // 2, 1, ROWS, LANES),
            second.reshape(INNER * LEFT // 2, 1, ROWS, LANES),
        ],
        axis=1,
    ).reshape(INNER * LEFT * ROWS, LANES)
    high = stacked.astype(jnp.bfloat16)
    low = (stacked - high.astype(jnp.float32)).astype(jnp.bfloat16)
    split = jnp.concatenate([high, low], axis=1)

    def tile_copy(spot):
        return pltpu.make_async_remote_copy(
            src_ref=s_out.at[spot],
            dst_ref=s_in.at[place],
            send_sem=s_send.at[spot],
            recv_sem=s_recv.at[place],
            device_id=tile_device(spot),
            device_id_type=MESH_ID,
        )

    def tile_arrival(spot):
        return pltpu.make_async_remote_copy(
            src_ref=s_out.at[spot],
            dst_ref=s_in.at[spot],
            send_sem=s_send.at[spot],
            recv_sem=s_recv.at[spot],
            device_id=tile_device(spot),
            device_id_type=MESH_ID,
        )

    chunks = 4
    per = GROUP // chunks
    lead = (z // (PLANES // chunks)) * per
    for chunk in range(chunks):
        base = pl.multiple_of((lead + (chunk + 2) % chunks * per) % GROUP, per)
        rows = pl.ds(pl.multiple_of(base * 2 * ROWS, LANES), per * 2 * ROWS)
        both = jnp.dot(kron[rows, :], split, preferred_element_type=jnp.float32)
        s_out[pl.ds(base, per)] = (
            (both[:, :LANES] + both[:, LANES:]).astype(jnp.bfloat16).reshape(per, 2 * ROWS, LANES)
        )

        @pl.loop(0, per)
        def _(step):
            spot = base + (step + place) % per

            @pl.when(spot != place)
            def _():
                tile_copy(spot).start()

    s_in[place] = s_out[place]
    own_r.wait()

    @pl.loop(1, GROUP)
    def _(step):
        tile_arrival((place + step) % GROUP).wait_recv()

    mixed = jnp.concatenate(
        [s_in[pl.ds(eight * 8, 8)].reshape(LANES, LANES) for eight in range(GROUP // 8)], axis=1
    )
    for side in range(2):
        columns = pl.ds(side * TILE, TILE)
        ladder = jnp.dot(mixed, r_all[:, columns], preferred_element_type=jnp.float32)
        ladder = ladder.reshape(8, 2, ROWS, TILE)[:, side]
        out_ref[:, columns] = ladder.reshape(8 * ROWS, TILE)

    for copies in ring:
        for copy in copies:
            copy.wait_send()
    for copy in near:
        copy.wait_send()

    @pl.loop(1, 2 * INNER)
    def _(step):
        mix_arrival((mix_place + step) % (2 * INNER)).wait_send()

    @pl.loop(1, GROUP)
    def _(step):
        tile_arrival((place + step) % GROUP).wait_send()


def on_device(amplitudes, left_factors, right_factors, tile_pattern, occupied_shift, virtual_shift):
    width = amplitudes.shape[1]
    out_width = right_factors.shape[1]
    ladder = pl.pallas_call(
        kernel,
        name="ladder",
        out_shape=jax.ShapeDtypeStruct((occupied_shift.shape[0], out_width), jnp.float32),
        in_specs=[pl.BlockSpec(memory_space=pl.ANY)] * 3
        + [pl.BlockSpec(memory_space=pltpu.VMEM)],
        out_specs=pl.BlockSpec(memory_space=pltpu.VMEM),
        scratch_shapes=[
            pltpu.VMEM((PLANES, ROWS, width), jnp.bfloat16),
            pltpu.VMEM((QUADS, DEPTH // QUADS, width), jnp.bfloat16),
            pltpu.VMEM(right_factors.shape, jnp.bfloat16),
            pltpu.VMEM((RIGHT * ROWS, 2 * LANES), jnp.bfloat16),
            pltpu.VMEM((2 * INNER, LEFT // 2, ROWS, LANES), jnp.float32),
            pltpu.VMEM((2 * INNER, LEFT // 2, ROWS, LANES), jnp.float32),
            pltpu.VMEM((GROUP, 2 * ROWS, LANES), jnp.bfloat16),
            pltpu.VMEM((GROUP, 2 * ROWS, LANES), jnp.bfloat16),
            pltpu.SemaphoreType.DMA((2, PLANES // 2, HALVES)),
            pltpu.SemaphoreType.DMA((2, PLANES // 2, HALVES)),
            pltpu.SemaphoreType.DMA((QUADS - 1,)),
            pltpu.SemaphoreType.DMA((QUADS - 1,)),
            pltpu.SemaphoreType.DMA((2 * INNER,)),
            pltpu.SemaphoreType.DMA((2 * INNER,)),
            pltpu.SemaphoreType.DMA((GROUP,)),
            pltpu.SemaphoreType.DMA((GROUP,)),
            pltpu.SemaphoreType.DMA((3,)),
        ],
        compiler_params=pltpu.CompilerParams(
            collective_id=0, has_side_effects=True, vmem_limit_bytes=32 << 20
        ),
    )(amplitudes, left_factors, right_factors, tile_pattern)
    return ladder / (occupied_shift[:, None] + virtual_shift[None, :])


def solution(mesh):
    torus = Mesh(
        mesh.devices.reshape(PLANES, 2, 2, mesh.shape["inner"]), (*TILE_AXES, "inner")
    )
    placed = (
        P(TILE_AXES, "inner"),
        P(TILE_AXES, "inner"),
        P(None, TILE_AXES),
        P(),
        P("inner"),
        P(TILE_AXES),
    )
    return jax.shard_map(
        on_device, mesh=torus, in_specs=placed, out_specs=P("inner", TILE_AXES), check_vma=False
    )
```

time: 223 us -> 72.3 us (0.32)
  waiting for transfers between devices: 119 us -> 0 us
  Pallas kernels: 0 us -> 67.2 us
  blocking collectives: 36.2 us -> 0 us
  matrix products: 19.9 us -> 0 us
  starting transfers between devices: 17 us -> 0 us
  between operations: 13.5 us -> 0.03 us
  local copies, waits for them, and re-layouts: 11.2 us -> 3.91 us
  loops' own time: 5.51 us -> 0 us
    pallas_call x0 -> x1, Pallas kernels: none -> 67.2 us  [on_device(): pl.pallas_call(kernel, name='ladder', out_shape=jax.ShapeDtypeStruct((occ...]
    all_gather x1 -> x0, waiting for transfers between devices: 59 us -> none  [on_device(): factor_block = lax.all_gather(left_factors, TILE_AXES, axis=0, tiled=True)]
    all_to_all x1 -> x0, waiting for transfers between devices: 59 us -> none  [copy_for_each(): lax.all_to_all(jnp.broadcast_to(shard[None], (peers, *shard.shape)), axis...]
    all_to_all x2 -> x0, blocking collectives: 36.2 us -> none  [the longest x1 27.4 us: sum_at_owner(): lax.all_to_all(pieces, axis, split_axis=0, concat_axis=0, tiled=True)]
    dot_general x7 -> x0, matrix products: 19.9 us -> none  [include(): jnp.dot(amplitude_tile, integral, preferred_element_type=jnp.float32)]
    all_to_all x1 -> x0, starting transfers between devices: 17 us -> none  [copy_for_each(): lax.all_to_all(jnp.broadcast_to(shard[None], (peers, *shard.shape)), axis...]
    dynamic_slice x9 -> x0, local copies, waits for them, and re-layouts: 5.57 us -> none  [the longest x8 4.8 us: visit_tile(): local_mask[left_slot, right_slot] != 0]
    another operation x9 -> x0, loops' own time: 5.51 us -> none  [the longest x1 5.32 us: on_device(): lax.fori_loop(0, left_tiles * right_tiles, visit_tile, jnp.zeros((gathere...]
  transfers between devices with their start and end apart: 2 -> 0, of which waited for: 2 -> 0; matrix products, arithmetic and copies ran while one was open for 2% -> 0% of each run, Pallas kernels for 0% -> 0%
where the time goes in v1:
time: 72.3 us; the launch traced here: 72 us
  Pallas kernels  67.2 us (93%)
  local copies, waits for them, and re-layouts  3.91 us (5%)
  other arithmetic  0.81 us (1%)
    pallas_call x1, Pallas kernels, on_device(): pl.pallas_call(kernel, name='ladder', out_shape=jax.ShapeDtypeStruct((occ...  67.2 us
    unnamed x12, local copies, waits for them, and re-layouts  3.91 us

profile of v1, /device:TPU:1, one launch (start us, length us, event | category | flops | bytes accessed | tf_op | source)
XLA Modules:
  0.0 72.0 jit_solution(16189003628482938310)
XLA Ops:
  0.0 0.0 copy-start
  0.0 1.6 %copy-done = bf16[1024,1024]{1,0:T(8,128)(2,1)S(1)} copy-done((bf16[1024,1024]{1,0:T(8,128)(2,1)S(1)}, bf16[1024,1024]{1,0:T(8,128)(2,1)}, u32[]{:S(2)}) %copy-start) | copy-done | bytes 2097176
  1.6 0.0 copy-start.1
  1.6 0.8 %copy-done.1 = bf16[16,2048]{1,0:T(8,128)(2,1)S(1)} copy-done((bf16[16,2048]{1,0:T(8,128)(2,1)S(1)}, bf16[16,2048]{1,0:T(8,128)(2,1)}, u32[]{:S(2)}) %copy-start.1) | copy-done | bytes 65560
  2.4 0.0 copy-start.2
  2.4 0.8 %copy-done.2 = bf16[8,2048]{1,0:T(8,128)(2,1)S(1)} copy-done((bf16[8,2048]{1,0:T(8,128)(2,1)S(1)}, bf16[8,2048]{1,0:T(8,128)(2,1)}, u32[]{:S(2)}) %copy-start.2) | copy-done | bytes 32792
  3.2 0.0 copy-start.3
  3.2 0.7 copy-done.3
  3.9 0.0 copy-start.4
  3.9 0.0 copy-start.5
  3.9 67.2 %ladder.1 = f32[64,1024]{1,0:T(8,128)S(1)} custom-call(bf16[8,2048]{1,0:T(8,128)(2,1)S(1)} %copy-done.2, bf16[16,2048]{1,0:T(8,128)(2,1)S(1)} %copy-done.1, bf16[1024,1024]{1,0:T(8,128)(2,1)S(1)} %copy-done, s32[32,128]{1,0:T(8,128)S(1)} %copy-done.3), custom_call_target="tpu_custom_call" | custom-call | tf_op jit(solution)/shard_map/ladder/pallas_call | solution.py:291
  71.2 0.0 copy-done.4
  71.2 0.0 copy-done.5
  71.2 0.8 %add_divide_fusion = f32[64,1024]{1,0:T(8,128)} fusion(f32[64,1024]{1,0:T(8,128)S(1)} %ladder.1, f32[1024]{0:T(1024)S(1)} %copy-done.4, f32[64]{0:T(128)S(1)} %copy-done.5), kind=kLoop, calls=%fused_computation | loop fusion | flops 131072 | bytes 528640 | tf_op jit(solution)/shard_map/div | solution.py:321
Async XLA Ops:
  0.0 1.6 %copy-start = (bf16[1024,1024]{1,0:T(8,128)(2,1)S(1)}, bf16[1024,1024]{1,0:T(8,128)(2,1)}, u32[]{:S(2)}) copy-start(bf16[1024,1024]{1,0:T(8,128)(2,1)} %r_ref.1) | copy-start | bytes 6291460
  1.6 0.8 %copy-start.1 = (bf16[16,2048]{1,0:T(8,128)(2,1)S(1)}, bf16[16,2048]{1,0:T(8,128)(2,1)}, u32[]{:S(2)}) copy-start(bf16[16,2048]{1,0:T(8,128)(2,1)} %l_ref.1) | copy-start | bytes 196612
  2.4 0.8 %copy-start.2 = (bf16[8,2048]{1,0:T(8,128)(2,1)S(1)}, bf16[8,2048]{1,0:T(8,128)(2,1)}, u32[]{:S(2)}) copy-start(bf16[8,2048]{1,0:T(8,128)(2,1)} %a_ref.1) | copy-start | bytes 98308
  3.2 0.7 copy-start.3
  3.9 67.3 %copy-start.4 = (f32[1024]{0:T(1024)S(1)}, f32[1024]{0:T(1024)}, u32[]{:S(2)}) copy-start(f32[1024]{0:T(1024)} %param.11) | copy-start | bytes 12292
  3.9 67.3 %copy-start.5 = (f32[64]{0:T(128)S(1)}, f32[64]{0:T(128)}, u32[]{:S(2)}) copy-start(f32[64]{0:T(128)} %param.10) | copy-start | bytes 772

commit v2 on v1

v2 whole, which is shorter than its diff:
```python
import jax
import jax.numpy as jnp
from jax import lax
from jax.experimental import pallas as pl
from jax.experimental.pallas import tpu as pltpu
from jax.sharding import Mesh
from jax.sharding import PartitionSpec as P

TILE = 512
TILE_AXES = ("z", "y", "core")
MESH_ID = pl.DeviceIdType.MESH
PLANES = 16
PAIRS = 8
INNER = 8
QUADS = 4
LEFT = 4
RIGHT = 128
ROWS = 8
DEPTH = 16
LANES = 128
GROUP = PLANES * QUADS
CHUNKS = 4
PER = GROUP // CHUNKS
LAG = 8
ORDER = (1, 7, 2, 6, 3, 5, 4)


def turn(step):
    return jnp.where(step % 2 == 1, (step + 1) // 2, (PAIRS - step // 2) % PAIRS)


def kernel(
    a_ref, l_ref, r_ref, pattern_ref, out_ref,
    a_all, l_all, r_all, pattern, kron, m_out, m_in, s_out, s_in,
    gather_send, gather_recv, near_send, near_recv, m_send, m_recv, s_send, s_recv, own_sem, ready,
):
    z = lax.axis_index("z")
    y = lax.axis_index("y")
    core = lax.axis_index("core")
    inner = lax.axis_index("inner")
    quad = y * 2 + core
    place = z * QUADS + quad
    pair = z // 2
    parity = z % 2

    def plane_device(plane):
        return dict(z=plane, y=y, core=core, inner=inner)

    def near_device(step):
        return dict(
            z=z,
            y=y if step == 1 else 1 - y,
            core=core if step == 2 else 1 - core,
            inner=inner,
        )

    def near_quad(step):
        return (y if step == 1 else 1 - y) * 2 + (core if step == 2 else 1 - core)

    def inner_device(other):
        return dict(z=z, y=y, core=core, inner=other)

    def tile_device(spot):
        return dict(z=spot >> 2, y=(spot >> 1) & 1, core=spot & 1, inner=inner)

    def greet(semaphore, device):
        pl.semaphore_signal(semaphore, 1, device_id=device, device_id_type=MESH_ID)

    barrier = pltpu.get_barrier_semaphore()
    for step in range(1, PLANES):
        greet(barrier, plane_device((z + step) % PLANES))
    for step in (1, 2, 3):
        greet(barrier, near_device(step))
    for step in range(1, INNER):
        greet(barrier, inner_device((inner + step) % INNER))

    own_a = pltpu.make_async_copy(a_ref, a_all.at[pair], own_sem.at[0])
    own_l = pltpu.make_async_copy(l_ref, l_all.at[parity, quad], own_sem.at[1])
    own_r = pltpu.make_async_copy(r_ref, r_all, own_sem.at[2])
    own_p = pltpu.make_async_copy(pattern_ref, pattern, own_sem.at[3])
    own_a.start()
    own_l.start()
    own_p.start()
    own_r.start()
    pl.semaphore_wait(barrier, PLANES - 1 + QUADS - 1 + INNER - 1)

    def factor_copy(src, side, step):
        spot = side * 4 + step
        mine = parity if side == 0 else 1 - parity
        return pltpu.make_async_remote_copy(
            src_ref=src,
            dst_ref=l_all.at[mine, quad],
            send_sem=near_send.at[spot],
            recv_sem=near_recv.at[spot],
            device_id=near_device(step) if step else plane_device(pair * 2 + 1 - parity),
            device_id_type=MESH_ID,
        )

    def factor_arrival(side, step):
        spot = side * 4 + step
        mine = parity if side == 0 else 1 - parity
        if step == 0:
            dst = l_all.at[1 - parity, quad]
        else:
            dst = l_all.at[mine, near_quad(step)]
        return pltpu.make_async_remote_copy(
            src_ref=l_ref,
            dst_ref=dst,
            send_sem=near_send.at[spot],
            recv_sem=near_recv.at[spot],
            device_id=plane_device(z),
            device_id_type=MESH_ID,
        )

    def gather_copy(step):
        return pltpu.make_async_remote_copy(
            src_ref=a_ref,
            dst_ref=a_all.at[pair],
            send_sem=gather_send.at[step],
            recv_sem=gather_recv.at[pair],
            device_id=plane_device((pair + step) % PAIRS * 2 + parity),
            device_id_type=MESH_ID,
        )

    def gather_arrival(source):
        return pltpu.make_async_remote_copy(
            src_ref=a_ref,
            dst_ref=a_all.at[source],
            send_sem=gather_send.at[0],
            recv_sem=gather_recv.at[source],
            device_id=plane_device(z),
            device_id_type=MESH_ID,
        )

    shared = [factor_copy(l_ref, 0, step) for step in range(4)]
    gathered = [gather_copy(step) for step in ORDER]
    for copy in shared + gathered:
        copy.start()
    for step in (1, 2, 3):
        greet(ready, near_device(step))

    own_p.wait()
    mask = jnp.where(pattern[...] != 0, 1.0, 0.0).astype(jnp.bfloat16)
    spread = jnp.where(
        lax.broadcasted_iota(jnp.int32, (32, 256), 0)
        == lax.broadcasted_iota(jnp.int32, (32, 256), 1) >> 3,
        1.0,
        0.0,
    ).astype(jnp.bfloat16)
    spread = lax.dot_general(
        mask, spread, (((0,), (0,)), ((), ())), preferred_element_type=jnp.float32
    ).astype(jnp.bfloat16)
    same = jnp.where(
        (lax.broadcasted_iota(jnp.int32, (LANES, 256), 0) & 7)
        == (lax.broadcasted_iota(jnp.int32, (LANES, 256), 1) & 7),
        1.0,
        0.0,
    )
    lifted = lax.broadcasted_iota(jnp.int32, (LANES, RIGHT), 1) - (
        lax.broadcasted_iota(jnp.int32, (LANES, RIGHT), 0) >> 3
    )

    @pl.loop(0, RIGHT // 16)
    def _(block):
        lift = jnp.where(lifted == block * 16, 1.0, 0.0).astype(jnp.bfloat16)
        rows = jnp.dot(lift, spread, preferred_element_type=jnp.float32)
        kron[pl.ds(pl.multiple_of(block * LANES, LANES), LANES), :] = (rows * same).astype(
            jnp.bfloat16
        )

    factor_arrival(0, 0).wait_recv()
    passed = [factor_copy(l_all.at[1 - parity, quad], 1, step) for step in (1, 2, 3)]
    for copy in passed:
        copy.start()
    own_a.wait()
    own_l.wait()
    for side in range(2):
        for step in (1, 2, 3):
            factor_arrival(side, step).wait_recv()

    def mix_copy(other):
        return pltpu.make_async_remote_copy(
            src_ref=m_out.at[other],
            dst_ref=m_in.at[inner],
            send_sem=m_send.at[other],
            recv_sem=m_recv.at[inner],
            device_id=inner_device(other),
            device_id_type=MESH_ID,
        )

    def mix_arrival(other):
        return pltpu.make_async_remote_copy(
            src_ref=m_out.at[other],
            dst_ref=m_in.at[other],
            send_sem=m_send.at[other],
            recv_sem=m_recv.at[other],
            device_id=inner_device(other),
            device_id_type=MESH_ID,
        )

    def tile_copy(spot):
        return pltpu.make_async_remote_copy(
            src_ref=s_out.at[spot],
            dst_ref=s_in.at[place],
            send_sem=s_send.at[spot],
            recv_sem=s_recv.at[place],
            device_id=tile_device(spot),
            device_id_type=MESH_ID,
        )

    def tile_arrival(spot):
        return pltpu.make_async_remote_copy(
            src_ref=s_out.at[spot],
            dst_ref=s_in.at[spot],
            send_sem=s_send.at[spot],
            recv_sem=s_recv.at[spot],
            device_id=tile_device(spot),
            device_id_type=MESH_ID,
        )

    lead = (z >> 2) * PER

    @pl.loop(0, PAIRS + LAG)
    def _(step):
        @pl.when(step < PAIRS)
        def _():
            other = (pair + turn(step)) % PAIRS

            @pl.when(step > 0)
            def _():
                gather_arrival(other).wait_recv()

            for left in range(LEFT):
                columns = pl.ds(left * TILE, TILE)
                m_out[other, left] = lax.dot_general(
                    a_all[other, :, columns],
                    l_all[:, :, :, columns].reshape(LANES, TILE),
                    (((1,), (1,)), ((), ())),
                    preferred_element_type=jnp.float32,
                )

            @pl.when(other != inner)
            def _():
                mix_copy(other).start()

            @pl.when(other == inner)
            def _():
                m_in[inner] = m_out[inner]

        @pl.when((step >= LAG) & ((pair + turn(step - LAG)) % PAIRS == inner))
        def _():
            pl.semaphore_wait(ready, QUADS - 1)

            @pl.loop(1, INNER)
            def _(more):
                mix_arrival((inner + more) % INNER).wait_recv()

            stacked = m_in[...].reshape(INNER * LEFT * ROWS, LANES)
            high = stacked.astype(jnp.bfloat16)
            low = (stacked - high.astype(jnp.float32)).astype(jnp.bfloat16)
            split = jnp.concatenate([high, low], axis=1)
            for chunk in range(CHUNKS):
                base = pl.multiple_of((lead + (chunk + 2) % CHUNKS * PER) % GROUP, PER)
                rows = pl.ds(pl.multiple_of(base * 2 * ROWS, LANES), PER * 2 * ROWS)
                both = jnp.dot(kron[rows, :], split, preferred_element_type=jnp.float32)
                both = both[:, :LANES] + both[:, LANES:]
                s_out[pl.ds(base, PER)] = both.astype(jnp.bfloat16).reshape(PER, 2 * ROWS, LANES)

                @pl.loop(0, PER)
                def _(more):
                    spot = base + ((more + place) & (PER - 1))

                    @pl.when(spot != place)
                    def _():
                        tile_copy(spot).start()

            s_in[place] = s_out[place]

    own_r.wait()

    @pl.loop(1, GROUP)
    def _(step):
        tile_arrival((place + step) & (GROUP - 1)).wait_recv()

    mixed = jnp.concatenate(
        [s_in[pl.ds(eight * 8, 8)].reshape(LANES, LANES) for eight in range(GROUP // 8)], axis=1
    )
    for side in range(2):
        columns = pl.ds(side * TILE, TILE)
        ladder = jnp.dot(mixed, r_all[:, columns], preferred_element_type=jnp.float32)
        ladder = ladder.reshape(8, 2, ROWS, TILE)[:, side]
        out_ref[:, columns] = ladder.reshape(8 * ROWS, TILE)

    for copy in shared + passed + gathered:
        copy.wait_send()

    @pl.loop(1, INNER)
    def _(step):
        mix_arrival((inner + step) % INNER).wait_send()

    @pl.loop(1, GROUP)
    def _(step):
        tile_arrival((place + step) & (GROUP - 1)).wait_send()


def on_device(amplitudes, left_factors, right_factors, tile_pattern, occupied_shift, virtual_shift):
    width = amplitudes.shape[1]
    out_width = right_factors.shape[1]
    operands = (amplitudes, left_factors, right_factors, tile_pattern)
    ladder = pl.pallas_call(
        kernel,
        name="ladder",
        out_shape=jax.ShapeDtypeStruct((occupied_shift.shape[0], out_width), jnp.float32),
        in_specs=[pl.BlockSpec(memory_space=pltpu.HBM)] * 4,
        out_specs=pl.BlockSpec(memory_space=pltpu.VMEM),
        scratch_shapes=[
            pltpu.VMEM((PAIRS, ROWS, width), jnp.bfloat16),
            pltpu.VMEM((2, QUADS, DEPTH, width), jnp.bfloat16),
            pltpu.VMEM(right_factors.shape, jnp.bfloat16),
            pltpu.VMEM(tile_pattern.shape, jnp.int32),
            pltpu.VMEM((RIGHT * ROWS, 2 * LANES), jnp.bfloat16),
            pltpu.VMEM((INNER, LEFT, ROWS, LANES), jnp.float32),
            pltpu.VMEM((INNER, LEFT, ROWS, LANES), jnp.float32),
            pltpu.VMEM((GROUP, 2 * ROWS, LANES), jnp.bfloat16),
            pltpu.VMEM((GROUP, 2 * ROWS, LANES), jnp.bfloat16),
            pltpu.SemaphoreType.DMA((PAIRS,)),
            pltpu.SemaphoreType.DMA((PAIRS,)),
            pltpu.SemaphoreType.DMA((8,)),
            pltpu.SemaphoreType.DMA((8,)),
            pltpu.SemaphoreType.DMA((INNER,)),
            pltpu.SemaphoreType.DMA((INNER,)),
            pltpu.SemaphoreType.DMA((GROUP,)),
            pltpu.SemaphoreType.DMA((GROUP,)),
            pltpu.SemaphoreType.DMA((4,)),
            pltpu.SemaphoreType.REGULAR,
        ],
        compiler_params=pltpu.CompilerParams(
            collective_id=0, has_side_effects=True, vmem_limit_bytes=16 << 20
        ),
    )(*(pltpu.with_memory_space_constraint(operand, pltpu.HBM) for operand in operands))
    return ladder / (occupied_shift[:, None] + virtual_shift[None, :])


def solution(mesh):
    torus = Mesh(
        mesh.devices.reshape(PLANES, 2, 2, mesh.shape["inner"]), (*TILE_AXES, "inner")
    )
    placed = (
        P(TILE_AXES, "inner"),
        P(TILE_AXES, "inner"),
        P(None, TILE_AXES),
        P(),
        P("inner"),
        P(TILE_AXES),
    )
    return jax.shard_map(
        on_device, mesh=torus, in_specs=placed, out_specs=P("inner", TILE_AXES), check_vma=False
    )
```

time: 72.3 us -> 55.1 us (0.76)
  Pallas kernels: 67.2 us -> 54.1 us
  local copies, waits for them, and re-layouts: 3.91 us -> 0.01 us
    pallas_call x1, Pallas kernels: 67.2 us -> 54.1 us  [on_device(): pl.pallas_call(kernel, name='ladder', out_shape=jax.ShapeDtypeStruct((occ...]
    unnamed x12 -> x4, local copies, waits for them, and re-layouts: 3.91 us -> 0.01 us
where the time goes in v2:
time: 55.1 us; the launch traced here: 55 us
  Pallas kernels  54.1 us (98%)
  other arithmetic  0.81 us (1%)
    pallas_call x1, Pallas kernels, on_device(): pl.pallas_call(kernel, name='ladder', out_shape=jax.ShapeDtypeStruct((occ...  54.1 us

profile of v2, /device:TPU:1, one launch (start us, length us, event | category | flops | bytes accessed | tf_op | source)
XLA Modules:
  0.0 55.0 jit_solution(4042164426591231626)
XLA Ops:
  0.0 0.0 copy-start
  0.0 0.0 copy-start.1
  0.0 54.1 %ladder.1 = f32[64,1024]{1,0:T(8,128)S(1)} custom-call(bf16[8,2048]{1,0:T(8,128)(2,1)} %a_ref.1, bf16[16,2048]{1,0:T(8,128)(2,1)} %l_ref.1, bf16[1024,1024]{1,0:T(8,128)(2,1)} %r_ref.1, s32[32,128]{1,0:T(8,128)} %pattern_ref.1), custom_call_target="tpu_custom_call" | custom-call | tf_op jit(solution)/shard_map/ladder/pallas_call | solution.py:310
  54.2 0.0 copy-done
  54.2 0.0 copy-done.1
  54.2 0.8 %add_divide_fusion = f32[64,1024]{1,0:T(8,128)} fusion(f32[64,1024]{1,0:T(8,128)S(1)} %ladder.1, f32[1024]{0:T(1024)S(1)} %copy-done, f32[64]{0:T(128)S(1)} %copy-done.1), kind=kLoop, calls=%fused_computation | loop fusion | flops 131072 | bytes 528640 | tf_op jit(solution)/shard_map/div | solution.py:341
Async XLA Ops:
  0.0 54.2 %copy-start = (f32[1024]{0:T(1024)S(1)}, f32[1024]{0:T(1024)}, u32[]{:S(2)}) copy-start(f32[1024]{0:T(1024)} %param.11) | copy-start | bytes 12292
  0.0 54.2 %copy-start.1 = (f32[64]{0:T(128)S(1)}, f32[64]{0:T(128)}, u32[]{:S(2)}) copy-start(f32[64]{0:T(128)} %param.10) | copy-start | bytes 772

commit v3 on v2

--- a/solution.py
+++ b/solution.py
@@ -21,12 +21,6 @@
 GROUP = PLANES * QUADS
 CHUNKS = 4
 PER = GROUP // CHUNKS
-LAG = 8
-ORDER = (1, 7, 2, 6, 3, 5, 4)
-
-
-def turn(step):
-    return jnp.where(step % 2 == 1, (step + 1) // 2, (PAIRS - step // 2) % PAIRS)
 
 
 def kernel(
@@ -67,8 +61,9 @@
         pl.semaphore_signal(semaphore, 1, device_id=device, device_id_type=MESH_ID)
 
     barrier = pltpu.get_barrier_semaphore()
-    for step in range(1, PLANES):
+    for step in (4, 12, 2, 14):
         greet(barrier, plane_device((z + step) % PLANES))
+    greet(barrier, plane_device(pair * 2 + 1 - parity))
     for step in (1, 2, 3):
         greet(barrier, near_device(step))
     for step in range(1, INNER):
@@ -82,7 +77,7 @@
     own_l.start()
     own_p.start()
     own_r.start()
-    pl.semaphore_wait(barrier, PLANES - 1 + QUADS - 1 + INNER - 1)
+    pl.semaphore_wait(barrier, 5 + QUADS - 1 + INNER - 1)
 
     def factor_copy(src, side, step):
         spot = side * 4 + step
@@ -112,33 +107,39 @@
             device_id_type=MESH_ID,
         )
 
-    def gather_copy(step):
-        return pltpu.make_async_remote_copy(
-            src_ref=a_ref,
-            dst_ref=a_all.at[pair],
-            send_sem=gather_send.at[step],
-            recv_sem=gather_recv.at[pair],
+    def gather_copy(slot, source, step, columns=slice(None), half=0):
+        return pltpu.make_async_remote_copy(
+            src_ref=(a_ref if source is pair else a_all.at[source]).at[:, columns],
+            dst_ref=a_all.at[source, :, columns],
+            send_sem=gather_send.at[slot],
+            recv_sem=gather_recv.at[source, half],
             device_id=plane_device((pair + step) % PAIRS * 2 + parity),
             device_id_type=MESH_ID,
         )
 
-    def gather_arrival(source):
-        return pltpu.make_async_remote_copy(
-            src_ref=a_ref,
-            dst_ref=a_all.at[source],
+    def gather_arrival(source, columns=slice(None), half=0):
+        return pltpu.make_async_remote_copy(
+            src_ref=a_ref.at[:, columns],
+            dst_ref=a_all.at[source, :, columns],
             send_sem=gather_send.at[0],
-            recv_sem=gather_recv.at[source],
+            recv_sem=gather_recv.at[source, half],
             device_id=plane_device(z),
             device_id_type=MESH_ID,
         )
 
+    width = a_ref.shape[1] // 2
+    halves = [pl.ds(half * width, width) for half in range(2)]
+
     shared = [factor_copy(l_ref, 0, step) for step in range(4)]
-    gathered = [gather_copy(step) for step in ORDER]
-    for copy in shared + gathered:
+    first = [
+        gather_copy(side * 2 + half, pair, step, halves[half], half)
+        for half in range(2)
+        for side, step in enumerate((2, 6))
+    ]
+    second = [gather_copy(4 + side, pair, step) for side, step in enumerate((1, 7))]
+    for copy in first + shared + second:
         copy.start()
-    for step in (1, 2, 3):
-        greet(ready, near_device(step))
-
+    gathered = first + second
     own_p.wait()
     mask = jnp.where(pattern[...] != 0, 1.0, 0.0).astype(jnp.bfloat16)
     spread = jnp.where(
@@ -172,6 +173,16 @@
     passed = [factor_copy(l_all.at[1 - parity, quad], 1, step) for step in (1, 2, 3)]
     for copy in passed:
         copy.start()
+    for half in range(2):
+        for side, (back, on, over) in enumerate(((6, 1, 2), (2, 7, 6))):
+            source = (pair + back) % PAIRS
+            gather_arrival(source, halves[half], half).wait_recv()
+            onward = [gather_copy(6 + side * 2 + half, source, on, halves[half], half)]
+            if half == side:
+                onward.append(gather_copy(10 + side, source, over, halves[half], half))
+            for copy in onward:
+                copy.start()
+            gathered.extend(onward)
     own_a.wait()
     own_l.wait()
     for side in range(2):
@@ -218,63 +229,60 @@
             device_id_type=MESH_ID,
         )
 
-    lead = (z >> 2) * PER
-
-    @pl.loop(0, PAIRS + LAG)
+    for step in (0, 2, 6, 1, 7, 3, 5, 4):
+        other = (pair + step) % PAIRS
+        if step in (3, 4, 5):
+            for half in range(2):
+                gather_arrival(other, halves[half], half).wait_recv()
+        elif step in (1, 7):
+            gather_arrival(other).wait_recv()
+        for left in range(LEFT):
+            columns = pl.ds(left * TILE, TILE)
+            m_out[other, left] = lax.dot_general(
+                a_all[other, :, columns],
+                l_all[:, :, :, columns].reshape(LANES, TILE),
+                (((1,), (1,)), ((), ())),
+                preferred_element_type=jnp.float32,
+            )
+
+        @pl.when(other != inner)
+        def _(other=other):
+            mix_copy(other).start()
+
+    for step in (1, 2, 3):
+        greet(ready, near_device(step))
+    m_in[inner] = m_out[inner]
+    pl.semaphore_wait(ready, QUADS - 1)
+
+    @pl.loop(1, INNER)
     def _(step):
-        @pl.when(step < PAIRS)
+        mix_arrival((inner + step) % INNER).wait_recv()
+
+    stacked = m_in[...].reshape(INNER * LEFT * ROWS, LANES)
+    high = stacked.astype(jnp.bfloat16)
+    low = (stacked - high.astype(jnp.float32)).astype(jnp.bfloat16)
+    split = jnp.concatenate([high, low], axis=1)
+    for chunk in range(CHUNKS):
+        rows = pl.ds(chunk * PER * 2 * ROWS, PER * 2 * ROWS)
+        both = jnp.dot(kron[rows, :], split, preferred_element_type=jnp.float32)
+        both = both[:, :LANES] + both[:, LANES:]
+        s_out[pl.ds(chunk * PER, PER)] = both.astype(jnp.bfloat16).reshape(PER, 2 * ROWS, LANES)
+
+    @pl.loop(0, PLANES)
+    def _(count):
+        plane = (count & 8) + ((z + count) & 7)
+
+        @pl.when(plane != z)
         def _():
-            other = (pair + turn(step)) % PAIRS
-
-            @pl.when(step > 0)
-            def _():
-                gather_arrival(other).wait_recv()
-
-            for left in range(LEFT):
-                columns = pl.ds(left * TILE, TILE)
-                m_out[other, left] = lax.dot_general(
-                    a_all[other, :, columns],
-                    l_all[:, :, :, columns].reshape(LANES, TILE),
-                    (((1,), (1,)), ((), ())),
-                    preferred_element_type=jnp.float32,
-                )
-
-            @pl.when(other != inner)
-            def _():
-                mix_copy(other).start()
-
-            @pl.when(other == inner)
-            def _():
-                m_in[inner] = m_out[inner]
-
-        @pl.when((step >= LAG) & ((pair + turn(step - LAG)) % PAIRS == inner))
+            for turned in range(QUADS):
+                tile_copy(plane * QUADS + (quad ^ turned)).start()
+
+        @pl.when(plane == z)
         def _():
-            pl.semaphore_wait(ready, QUADS - 1)
-
-            @pl.loop(1, INNER)
-            def _(more):
-                mix_arrival((inner + more) % INNER).wait_recv()
-
-            stacked = m_in[...].reshape(INNER * LEFT * ROWS, LANES)
-            high = stacked.astype(jnp.bfloat16)
-            low = (stacked - high.astype(jnp.float32)).astype(jnp.bfloat16)
-            split = jnp.concatenate([high, low], axis=1)
-            for chunk in range(CHUNKS):
-                base = pl.multiple_of((lead + (chunk + 2) % CHUNKS * PER) % GROUP, PER)
-                rows = pl.ds(pl.multiple_of(base * 2 * ROWS, LANES), PER * 2 * ROWS)
-                both = jnp.dot(kron[rows, :], split, preferred_element_type=jnp.float32)
-                both = both[:, :LANES] + both[:, LANES:]
-                s_out[pl.ds(base, PER)] = both.astype(jnp.bfloat16).reshape(PER, 2 * ROWS, LANES)
-
-                @pl.loop(0, PER)
-                def _(more):
-                    spot = base + ((more + place) & (PER - 1))
-
-                    @pl.when(spot != place)
-                    def _():
-                        tile_copy(spot).start()
-
-            s_in[place] = s_out[place]
+            for turned in range(1, QUADS):
+                tile_copy(plane * QUADS + (quad ^ turned)).start()
+
+    s_in[place] = s_out[place]
 
     own_r.wait()
 
@@ -323,8 +331,8 @@
             pltpu.VMEM((INNER, LEFT, ROWS, LANES), jnp.float32),
             pltpu.VMEM((GROUP, 2 * ROWS, LANES), jnp.bfloat16),
             pltpu.VMEM((GROUP, 2 * ROWS, LANES), jnp.bfloat16),
-            pltpu.SemaphoreType.DMA((PAIRS,)),
-            pltpu.SemaphoreType.DMA((PAIRS,)),
+            pltpu.SemaphoreType.DMA((12,)),
+            pltpu.SemaphoreType.DMA((PAIRS, 2)),
             pltpu.SemaphoreType.DMA((8,)),
             pltpu.SemaphoreType.DMA((8,)),
             pltpu.SemaphoreType.DMA((INNER,)),

time: 55.1 us -> 47.7 us (0.87)
  the two profiles are of different devices: /device:TPU:1 before, /device:TPU:137 now
where the time goes in v3:
time: 47.7 us; the launch traced here: 47.5 us
  Pallas kernels  46.7 us (98%)
  other arithmetic  0.81 us (2%)
    pallas_call x1, Pallas kernels, on_device(): pl.pallas_call(kernel, name='ladder', out_shape=jax.ShapeDtypeStruct((occ...  46.7 us

profile of v3, /device:TPU:137, one launch (start us, length us, event | category | flops | bytes accessed | tf_op | source)
XLA Modules:
  0.0 47.5 jit_solution(9789199823650948120)
XLA Ops:
  0.0 0.0 copy-start
  0.0 0.0 copy-start.1
  0.0 46.7 %ladder.1 = f32[64,1024]{1,0:T(8,128)S(1)} custom-call(bf16[8,2048]{1,0:T(8,128)(2,1)} %a_ref.1, bf16[16,2048]{1,0:T(8,128)(2,1)} %l_ref.1, bf16[1024,1024]{1,0:T(8,128)(2,1)} %r_ref.1, s32[32,128]{1,0:T(8,128)} %pattern_ref.1), custom_call_target="tpu_custom_call" | custom-call | tf_op jit(solution)/shard_map/ladder/pallas_call | solution.py:318
  46.7 0.0 copy-done
  46.7 0.0 copy-done.1
  46.7 0.8 %add_divide_fusion = f32[64,1024]{1,0:T(8,128)} fusion(f32[64,1024]{1,0:T(8,128)S(1)} %ladder.1, f32[1024]{0:T(1024)S(1)} %copy-done, f32[64]{0:T(128)S(1)} %copy-done.1), kind=kLoop, calls=%fused_computation | loop fusion | flops 131072 | bytes 528640 | tf_op jit(solution)/shard_map/div | solution.py:349
Async XLA Ops:
  0.0 46.7 %copy-start = (f32[1024]{0:T(1024)S(1)}, f32[1024]{0:T(1024)}, u32[]{:S(2)}) copy-start(f32[1024]{0:T(1024)} %param.11) | copy-start | bytes 12292
  0.0 46.7 %copy-start.1 = (f32[64]{0:T(128)S(1)}, f32[64]{0:T(128)}, u32[]{:S(2)}) copy-start(f32[64]{0:T(128)} %param.10) | copy-start | bytes 772

commit v4 on v3

--- a/solution.py
+++ b/solution.py
@@ -77,69 +77,6 @@
     own_l.start()
     own_p.start()
     own_r.start()
-    pl.semaphore_wait(barrier, 5 + QUADS - 1 + INNER - 1)
-
-    def factor_copy(src, side, step):
-        spot = side * 4 + step
-        mine = parity if side == 0 else 1 - parity
-        return pltpu.make_async_remote_copy(
-            src_ref=src,
-            dst_ref=l_all.at[mine, quad],
-            send_sem=near_send.at[spot],
-            recv_sem=near_recv.at[spot],
-            device_id=near_device(step) if step else plane_device(pair * 2 + 1 - parity),
-            device_id_type=MESH_ID,
-        )
-
-    def factor_arrival(side, step):
-        spot = side * 4 + step
-        mine = parity if side == 0 else 1 - parity
-        if step == 0:
-            dst = l_all.at[1 - parity, quad]
-        else:
-            dst = l_all.at[mine, near_quad(step)]
-        return pltpu.make_async_remote_copy(
-            src_ref=l_ref,
-            dst_ref=dst,
-            send_sem=near_send.at[spot],
-            recv_sem=near_recv.at[spot],
-            device_id=plane_device(z),
-            device_id_type=MESH_ID,
-        )
-
-    def gather_copy(slot, source, step, columns=slice(None), half=0):
-        return pltpu.make_async_remote_copy(
-            src_ref=(a_ref if source is pair else a_all.at[source]).at[:, columns],
-            dst_ref=a_all.at[source, :, columns],
-            send_sem=gather_send.at[slot],
-            recv_sem=gather_recv.at[source, half],
-            device_id=plane_device((pair + step) % PAIRS * 2 + parity),
-            device_id_type=MESH_ID,
-        )
-
-    def gather_arrival(source, columns=slice(None), half=0):
-        return pltpu.make_async_remote_copy(
-            src_ref=a_ref.at[:, columns],
-            dst_ref=a_all.at[source, :, columns],
-            send_sem=gather_send.at[0],
-            recv_sem=gather_recv.at[source, half],
-            device_id=plane_device(z),
-            device_id_type=MESH_ID,
-        )
-
-    width = a_ref.shape[1] // 2
-    halves = [pl.ds(half * width, width) for half in range(2)]
-
-    shared = [factor_copy(l_ref, 0, step) for step in range(4)]
-    first = [
-        gather_copy(side * 2 + half, pair, step, halves[half], half)
-        for half in range(2)
-        for side, step in enumerate((2, 6))
-    ]
-    second = [gather_copy(4 + side, pair, step) for side, step in enumerate((1, 7))]
-    for copy in first + shared + second:
-        copy.start()
-    gathered = first + second
     own_p.wait()
     mask = jnp.where(pattern[...] != 0, 1.0, 0.0).astype(jnp.bfloat16)
     spread = jnp.where(
@@ -169,6 +106,69 @@
             jnp.bfloat16
         )
 
+    pl.semaphore_wait(barrier, 5 + QUADS - 1 + INNER - 1)
+
+    def factor_copy(src, side, step):
+        spot = side * 4 + step
+        mine = parity if side == 0 else 1 - parity
+        return pltpu.make_async_remote_copy(
+            src_ref=src,
+            dst_ref=l_all.at[mine, quad],
+            send_sem=near_send.at[spot],
+            recv_sem=near_recv.at[spot],
+            device_id=near_device(step) if step else plane_device(pair * 2 + 1 - parity),
+            device_id_type=MESH_ID,
+        )
+
+    def factor_arrival(side, step):
+        spot = side * 4 + step
+        mine = parity if side == 0 else 1 - parity
+        if step == 0:
+            dst = l_all.at[1 - parity, quad]
+        else:
+            dst = l_all.at[mine, near_quad(step)]
+        return pltpu.make_async_remote_copy(
+            src_ref=l_ref,
+            dst_ref=dst,
+            send_sem=near_send.at[spot],
+            recv_sem=near_recv.at[spot],
+            device_id=plane_device(z),
+            device_id_type=MESH_ID,
+        )
+
+    def gather_copy(slot, source, step, columns=slice(None), half=0):
+        return pltpu.make_async_remote_copy(
+            src_ref=(a_ref if source is pair else a_all.at[source]).at[:, columns],
+            dst_ref=a_all.at[source, :, columns],
+            send_sem=gather_send.at[slot],
+            recv_sem=gather_recv.at[source, half],
+            device_id=plane_device((pair + step) % PAIRS * 2 + parity),
+            device_id_type=MESH_ID,
+        )
+
+    def gather_arrival(source, columns=slice(None), half=0):
+        return pltpu.make_async_remote_copy(
+            src_ref=a_ref.at[:, columns],
+            dst_ref=a_all.at[source, :, columns],
+            send_sem=gather_send.at[0],
+            recv_sem=gather_recv.at[source, half],
+            device_id=plane_device(z),
+            device_id_type=MESH_ID,
+        )
+
+    width = a_ref.shape[1] // 2
+    halves = [pl.ds(half * width, width) for half in range(2)]
+
+    shared = [factor_copy(l_ref, 0, step) for step in range(4)]
+    first = [
+        gather_copy(side * 2 + half, pair, step, halves[half], half)
+        for half in range(2)
+        for side, step in enumerate((2, 6))
+    ]
+    second = [gather_copy(4 + side, pair, step) for side, step in enumerate((1, 7))]
+    for copy in first + shared + second:
+        copy.start()
+    gathered = first + second
     factor_arrival(0, 0).wait_recv()
     passed = [factor_copy(l_all.at[1 - parity, quad], 1, step) for step in (1, 2, 3)]
     for copy in passed:
@@ -178,11 +178,16 @@
             source = (pair + back) % PAIRS
             gather_arrival(source, halves[half], half).wait_recv()
             onward = [gather_copy(6 + side * 2 + half, source, on, halves[half], half)]
-            if half == side:
-                onward.append(gather_copy(10 + side, source, over, halves[half], half))
             for copy in onward:
                 copy.start()
             gathered.extend(onward)
+    for side, (back, over) in enumerate(((5, 1), (3, 7))):
+        source = (pair + back) % PAIRS
+        gather_arrival(source, halves[side], side).wait_recv()
+        onward = gather_copy(10 + side, source, over, halves[side], side)
+        onward.start()
+        gathered.append(onward)
+
     own_a.wait()
     own_l.wait()
     for side in range(2):
@@ -232,7 +237,7 @@
     for step in (0, 2, 6, 1, 7, 3, 5, 4):
         other = (pair + step) % PAIRS
         if step in (3, 4, 5):
-            for half in range(2):
+            for half in ((0, 1) if step == 4 else (0,) if step == 3 else (1,)):
                 gather_arrival(other, halves[half], half).wait_recv()
         elif step in (1, 7):
             gather_arrival(other).wait_recv()

time: 47.7 us -> 47.8 us (level)
  the two profiles are of different devices: /device:TPU:137 before, /device:TPU:1 now
where the time goes in v4:
time: 47.8 us; the launch traced here: 47.7 us
  Pallas kernels  46.8 us (98%)
  other arithmetic  0.81 us (2%)
    pallas_call x1, Pallas kernels, on_device(): pl.pallas_call(kernel, name='ladder', out_shape=jax.ShapeDtypeStruct((occ...  46.8 us

profile of v4, /device:TPU:1, one launch (start us, length us, event | category | flops | bytes accessed | tf_op | source)
XLA Modules:
  0.0 47.7 jit_solution(12408030133285537864)
XLA Ops:
  0.0 0.0 copy-start
  0.0 0.0 copy-start.1
  0.0 46.8 %ladder.1 = f32[64,1024]{1,0:T(8,128)S(1)} custom-call(bf16[8,2048]{1,0:T(8,128)(2,1)} %a_ref.1, bf16[16,2048]{1,0:T(8,128)(2,1)} %l_ref.1, bf16[1024,1024]{1,0:T(8,128)(2,1)} %r_ref.1, s32[32,128]{1,0:T(8,128)} %pattern_ref.1), custom_call_target="tpu_custom_call" | custom-call | tf_op jit(solution)/shard_map/ladder/pallas_call | solution.py:323
  46.8 0.0 copy-done
  46.8 0.0 copy-done.1
  46.8 0.8 %add_divide_fusion = f32[64,1024]{1,0:T(8,128)} fusion(f32[64,1024]{1,0:T(8,128)S(1)} %ladder.1, f32[1024]{0:T(1024)S(1)} %copy-done, f32[64]{0:T(128)S(1)} %copy-done.1), kind=kLoop, calls=%fused_computation | loop fusion | flops 131072 | bytes 528640 | tf_op jit(solution)/shard_map/div | solution.py:354
Async XLA Ops:
  0.0 46.8 %copy-start = (f32[1024]{0:T(1024)S(1)}, f32[1024]{0:T(1024)}, u32[]{:S(2)}) copy-start(f32[1024]{0:T(1024)} %param.11) | copy-start | bytes 12292
  0.0 46.8 %copy-start.1 = (f32[64]{0:T(128)S(1)}, f32[64]{0:T(128)}, u32[]{:S(2)}) copy-start(f32[64]{0:T(128)} %param.10) | copy-start | bytes 772

commit v5 on v4

--- a/solution.py
+++ b/solution.py
@@ -291,18 +291,25 @@
 
     own_r.wait()
 
-    @pl.loop(1, GROUP)
-    def _(step):
-        tile_arrival((place + step) & (GROUP - 1)).wait_recv()
-
-    mixed = jnp.concatenate(
-        [s_in[pl.ds(eight * 8, 8)].reshape(LANES, LANES) for eight in range(GROUP // 8)], axis=1
-    )
-    for side in range(2):
-        columns = pl.ds(side * TILE, TILE)
-        ladder = jnp.dot(mixed, r_all[:, columns], preferred_element_type=jnp.float32)
-        ladder = ladder.reshape(8, 2, ROWS, TILE)[:, side]
-        out_ref[:, columns] = ladder.reshape(8 * ROWS, TILE)
+    span = GROUP // 2
+    for part in range(2):
+
+        @pl.loop(part * span, part * span + span)
+        def _(spot):
+            @pl.when(spot != place)
+            def _():
+                tile_arrival(spot).wait_recv()
+
+        mixed = jnp.concatenate(
+            [s_in[pl.ds(part * span + eight * 8, 8)].reshape(LANES, LANES) for eight in range(span // 8)],
+            axis=1,
+        )
+        depths = pl.ds(part * TILE, TILE)
+        for side in range(2):
+            columns = pl.ds(side * TILE, TILE)
+            ladder = jnp.dot(mixed, r_all[depths, columns], preferred_element_type=jnp.float32)
+            ladder = ladder.reshape(8, 2, ROWS, TILE)[:, side].reshape(8 * ROWS, TILE)
+            out_ref[:, columns] = ladder if part == 0 else out_ref[:, columns] + ladder
 
     for copy in shared + passed + gathered:
         copy.wait_send()

time: 47.8 us -> 47.6 us (level)
  no operation moved by 1% of the time
where the time goes in v5:
time: 47.6 us; the launch traced here: 47.5 us
  Pallas kernels  46.7 us (98%)
  other arithmetic  0.81 us (2%)
    pallas_call x1, Pallas kernels, on_device(): pl.pallas_call(kernel, name='ladder', out_shape=jax.ShapeDtypeStruct((occ...  46.7 us

profile of v5, /device:TPU:1, one launch (start us, length us, event | category | flops | bytes accessed | tf_op | source)
XLA Modules:
  0.0 47.5 jit_solution(3582273093558111556)
XLA Ops:
  0.0 0.0 copy-start
  0.0 0.0 copy-start.1
  0.0 46.7 %ladder.1 = f32[64,1024]{1,0:T(8,128)S(1)} custom-call(bf16[8,2048]{1,0:T(8,128)(2,1)} %a_ref.1, bf16[16,2048]{1,0:T(8,128)(2,1)} %l_ref.1, bf16[1024,1024]{1,0:T(8,128)(2,1)} %r_ref.1, s32[32,128]{1,0:T(8,128)} %pattern_ref.1), custom_call_target="tpu_custom_call" | custom-call | tf_op jit(solution)/shard_map/ladder/pallas_call | solution.py:330
  46.7 0.0 copy-done
  46.7 0.0 copy-done.1
  46.7 0.8 %add_divide_fusion = f32[64,1024]{1,0:T(8,128)} fusion(f32[64,1024]{1,0:T(8,128)S(1)} %ladder.1, f32[1024]{0:T(1024)S(1)} %copy-done, f32[64]{0:T(128)S(1)} %copy-done.1), kind=kLoop, calls=%fused_computation | loop fusion | flops 131072 | bytes 528640 | tf_op jit(solution)/shard_map/div | solution.py:361
Async XLA Ops:
  0.0 46.7 %copy-start = (f32[1024]{0:T(1024)S(1)}, f32[1024]{0:T(1024)}, u32[]{:S(2)}) copy-start(f32[1024]{0:T(1024)} %param.11) | copy-start | bytes 12292
  0.0 46.7 %copy-start.1 = (f32[64]{0:T(128)S(1)}, f32[64]{0:T(128)}, u32[]{:S(2)}) copy-start(f32[64]{0:T(128)} %param.10) | copy-start | bytes 772

commit v6 on v5

--- a/solution.py
+++ b/solution.py
@@ -61,13 +61,13 @@
         pl.semaphore_signal(semaphore, 1, device_id=device, device_id_type=MESH_ID)
 
     barrier = pltpu.get_barrier_semaphore()
+    for step in range(1, INNER):
+        greet(barrier, inner_device((inner + step) % INNER))
     for step in (4, 12, 2, 14):
         greet(barrier, plane_device((z + step) % PLANES))
     greet(barrier, plane_device(pair * 2 + 1 - parity))
     for step in (1, 2, 3):
         greet(barrier, near_device(step))
-    for step in range(1, INNER):
-        greet(barrier, inner_device((inner + step) % INNER))
 
     own_a = pltpu.make_async_copy(a_ref, a_all.at[pair], own_sem.at[0])
     own_l = pltpu.make_async_copy(l_ref, l_all.at[parity, quad], own_sem.at[1])

time: 47.6 us -> 47.4 us (level)
  no operation moved by 1% of the time
where the time goes in v6:
time: 47.4 us; the launch traced here: 47.3 us
  Pallas kernels  46.5 us (98%)
  other arithmetic  0.81 us (2%)
    pallas_call x1, Pallas kernels, on_device(): pl.pallas_call(kernel, name='ladder', out_shape=jax.ShapeDtypeStruct((occ...  46.5 us

profile of v6, /device:TPU:1, one launch (start us, length us, event | category | flops | bytes accessed | tf_op | source)
XLA Modules:
  0.0 47.3 jit_solution(8067551376483518801)
XLA Ops:
  0.0 0.0 copy-start
  0.0 0.0 copy-start.1
  0.0 46.5 %ladder.1 = f32[64,1024]{1,0:T(8,128)S(1)} custom-call(bf16[8,2048]{1,0:T(8,128)(2,1)} %a_ref.1, bf16[16,2048]{1,0:T(8,128)(2,1)} %l_ref.1, bf16[1024,1024]{1,0:T(8,128)(2,1)} %r_ref.1, s32[32,128]{1,0:T(8,128)} %pattern_ref.1), custom_call_target="tpu_custom_call" | custom-call | tf_op jit(solution)/shard_map/ladder/pallas_call | solution.py:330
  46.5 0.0 copy-done
  46.5 0.0 copy-done.1
  46.5 0.8 %add_divide_fusion = f32[64,1024]{1,0:T(8,128)} fusion(f32[64,1024]{1,0:T(8,128)S(1)} %ladder.1, f32[1024]{0:T(1024)S(1)} %copy-done, f32[64]{0:T(128)S(1)} %copy-done.1), kind=kLoop, calls=%fused_computation | loop fusion | flops 131072 | bytes 528640 | tf_op jit(solution)/shard_map/div | solution.py:361
Async XLA Ops:
  0.0 46.5 %copy-start = (f32[1024]{0:T(1024)S(1)}, f32[1024]{0:T(1024)}, u32[]{:S(2)}) copy-start(f32[1024]{0:T(1024)} %param.11) | copy-start | bytes 12292
  0.0 46.5 %copy-start.1 = (f32[64]{0:T(128)S(1)}, f32[64]{0:T(128)}, u32[]{:S(2)}) copy-start(f32[64]{0:T(128)} %param.10) | copy-start | bytes 772
